TPU v7x, 32 devices: a whole 2x2x4 slice. The times are simulated.
32 devices in a mesh: req: 16 (over z, x, core), tp: 2 (over y).
Axes of the slice: x: 2, y: 2, z: 4, core: 2. Of those that a mesh axis runs over, the one named last changes fastest.
Arguments:
- state: bfloat16 [256, 2048], P('req'), may hold values from -3 to 3
- norm_gain: float32 [2048], replicated, may hold values from 0.25 to 4
- w_qkv: bfloat16 [2048, 2, 512], P(None, 'tp'), may hold values from -0.125 to 0.125
- w_out: bfloat16 [2, 256, 2048], P('tp'), may hold values from -0.25 to 0.25
- kv_cache: bfloat16 [2944, 2, 16, 256], P('req', 'tp')
- lengths: int32 [256], P('req'), may hold values from 32 to 1024, as said below
- page_table: int32 [256, 64], P('req'), may hold values from 0 to 183, as said below
- dest_slot: int32 [256], P('req'), may hold values from 0 to 255, as said below
Outputs:
- new_state: bfloat16 [256, 2048], P('req')
Inputs may be any that keep to these rules, and one draw needn't show every extreme that they name: `lengths`: each device of req holds at most one request with more than 128 cached tokens; all others have 32 to 128; in every draw some request has exactly 1024. `page_table`: entry j of row r, for j below ceil(lengths[r] / 16), is the page (numbered within the home device r // 16) holding tokens j * 16 to (j + 1) * 16 - 1 of request r; no page serves two such entries; the entries after those are 183. dest_slot is a permutation. The request in slot k of device i of req (index i * 16 + k) goes to slot k of device (i + o_k) mod (16), with offsets o_k the same for all devices; at most 2 requests of one device go to one device, and exactly 2 do for some pairs.
All inputs are finite; a program needn't handle non-finite values.
Results may differ from a plain program's by a relative error of at most 0.01.
Values may be sent and summed in bfloat16 or wider, within the bound.
A program may use at most 64 MiB of HBM per device.

v0:
```python
import jax
import jax.numpy as jnp
from jax import lax
from jax.sharding import PartitionSpec as P


def normalize(values, scale_gain):
    wide = values.astype(jnp.float32)
    factor = lax.rsqrt(jnp.mean(wide * wide, axis=-1, keepdims=True) + 1e-05)
    return (wide * factor * scale_gain).astype(jnp.bfloat16)


def rotate(values, positions):
    half_size = values.shape[-1] // 2
    freqs = jnp.exp(
        -jnp.log(1000000.0) * 2.0 * jnp.arange(half_size, dtype=jnp.float32) / (2 * half_size)
    )
    angles = positions.astype(jnp.float32)[:, None, None] * freqs
    cosine = jnp.cos(angles)
    sine = jnp.sin(angles)
    first = values[..., :half_size]
    second = values[..., half_size:]
    return jnp.concatenate(
        [first * cosine - second * sine, second * cosine + first * sine], axis=-1
    )


def attend(query, new_key, new_value, page_pool, lengths, page_table):
    row_count = query.shape[0]
    group_size = query.shape[1]
    head_size = query.shape[2]
    page_count = page_pool.shape[0]
    page_size = page_pool.shape[1]
    table_width = page_table.shape[1]
    scale = 1.0 / jnp.sqrt(jnp.float32(head_size))
    used_pages = (lengths + page_size - 1) // page_size
    valid = jnp.arange(table_width, dtype=jnp.int32)[None, :] < used_pages[:, None]
    matches = (
        page_table[:, :, None] == jnp.arange(page_count, dtype=jnp.int32)[None, None, :]
    ) & valid[:, :, None]
    owner_int = jnp.sum(matches.astype(jnp.int32), axis=1)
    owner = owner_int.astype(jnp.float32)
    offsets = (jnp.arange(table_width, dtype=jnp.int32) * page_size)[None, :, None]
    page_base = jnp.sum(matches.astype(jnp.int32) * offsets, axis=(0, 1))
    page_limit = jnp.sum(owner_int * lengths[:, None], axis=0)
    live = (
        page_base[:, None] + jnp.arange(page_size, dtype=jnp.int32)[None, :] < page_limit[:, None]
    )
    page_query = jnp.dot(
        owner.T.astype(jnp.bfloat16),
        query.reshape(row_count, group_size * head_size),
        preferred_element_type=jnp.float32,
    )
    page_query = page_query.astype(jnp.bfloat16).reshape(page_count, group_size, head_size)
    scores = (
        jnp.einsum(
            "pjc,ptc->pjt",
            page_query,
            page_pool[:, :, :head_size],
            preferred_element_type=jnp.float32,
        )
        * scale
    )
    scores = jnp.where(live[:, None, :], scores, -jnp.inf)
    score_new = jnp.einsum("rjc,rc->rj", query, new_key, preferred_element_type=jnp.float32) * scale
    page_top = jnp.max(scores, axis=-1)
    row_top = jnp.max(jnp.where(owner_int[:, :, None] > 0, page_top[None, :, :], -jnp.inf), axis=1)
    row_top = jnp.maximum(row_top, score_new)
    spread_top = jnp.dot(owner.T, row_top, precision=lax.Precision.HIGHEST)
    weights = jnp.exp(scores - spread_top[:, :, None])
    weight_new = jnp.exp(score_new - row_top)
    total = jnp.dot(owner, jnp.sum(weights, axis=-1), precision=lax.Precision.HIGHEST) + weight_new
    page_sums = jnp.einsum(
        "pjt,ptc->pjc",
        weights.astype(jnp.bfloat16),
        page_pool[:, :, head_size:],
        preferred_element_type=jnp.float32,
    )
    numer = jnp.dot(
        owner,
        page_sums.reshape(page_count, group_size * head_size),
        precision=lax.Precision.HIGHEST,
    )
    numer = numer.reshape(row_count, group_size, head_size)
    numer = (
        numer
        + weight_new.astype(jnp.bfloat16).astype(jnp.float32)[:, :, None]
        * new_value.astype(jnp.float32)[:, None, :]
    )
    return (
        (numer / total[:, :, None]).astype(jnp.bfloat16).reshape(row_count, group_size * head_size)
    )


def relocate(mixed, dest_slot):
    row_count = mixed.shape[0]
    device_count = lax.axis_size("req")
    own_index = lax.axis_index("req")
    target_device = dest_slot // row_count
    shift_amount = (target_device - own_index) % device_count
    collected = lax.all_gather(mixed, "req", axis=0, tiled=True)
    source_device = (own_index - shift_amount) % device_count
    source_rows = source_device * row_count + jnp.arange(row_count, dtype=jnp.int32)
    return jnp.take(collected, source_rows, axis=0)


def local(state, norm_gain, w_qkv, w_out, kv_cache, lengths, page_table, dest_slot):
    row_count = state.shape[0]
    width = state.shape[1]
    head_size = kv_cache.shape[3] // 2
    group_size = w_out.shape[1] // head_size
    normed = normalize(state, norm_gain)
    proj = jnp.dot(normed, w_qkv.reshape(width, w_qkv.shape[2]), preferred_element_type=jnp.float32)
    query = rotate(
        proj[:, : group_size * head_size].reshape(row_count, group_size, head_size), lengths
    ).astype(jnp.bfloat16)
    new_key = rotate(proj[:, None, group_size * head_size : (group_size + 1) * head_size], lengths)[
        :, 0
    ].astype(jnp.bfloat16)
    new_value = proj[:, (group_size + 1) * head_size :].astype(jnp.bfloat16)
    attn = attend(query, new_key, new_value, kv_cache[:, 0], lengths, page_table)
    partial_out = jnp.dot(attn, w_out[0], preferred_element_type=jnp.float32)
    summed = lax.psum(partial_out, "tp")
    mixed = (state.astype(jnp.float32) + summed).astype(jnp.bfloat16)
    return relocate(mixed, dest_slot)


def solution(mesh):
    placed = (
        P("req", None),
        P(),
        P(None, "tp", None),
        P("tp", None, None),
        P("req", "tp", None, None),
        P("req"),
        P("req", None),
        P("req"),
    )
    return jax.shard_map(
        local, mesh=mesh, in_specs=placed, out_specs=P("req", None), check_vma=False
    )
```

profile of v0, /device:TPU:0, one launch (start us, length us, event | category | flops | bytes accessed | tf_op | source)
XLA Modules:
  0.0 92.7 jit_solution(18286603399373292580)
XLA Ops:
  6.5 0.0 copy-start
  6.5 0.0 all-reduce.2.cloned.1.call-start
  6.6 0.8 fusion.54
  7.4 0.1 iota_compare_fusion.1
  7.5 1.2 %select_reduce_fusion = (s32[184]{0:T(256)S(1)}, s32[16,184]{1,0:T(8,128)S(1)}) fusion(s32[64]{0:T(128)S(1)} %iota_multiply_fusion, s32[16,64]{1,0:T(8,128)} %param.14, pred[16,64]{1,0:T(8,128)(4,1)S(1)} %iota_compare_fusion.1), kind=kLoop, calls=%fused_computation.13 | loop fusion | flops 1127368 | bytes 17888 | tf_op jit(solution)/shard_map/reduce_sum | solution.py:44
  8.7 0.7 multiply_reduce_fusion
  9.4 1.0 %fusion.14 = f32[16]{0:T(128)S(1)} fusion(bf16[16,2048]{1,0:T(8,128)(2,1)} %param.8), kind=kLoop, calls=%fused_computation.27 | loop fusion | flops 98288 | bytes 65600 | tf_op jit(solution)/shard_map/reduce_sum | solution.py:9
  10.4 0.0 copy-done
  10.4 1.3 %fusion = f32[16,512]{1,0:T(8,128)S(1)} fusion(bf16[2048,1,512]{2,0,1:T(8,128)(2,1)S(1)} %copy-done, bf16[16,2048]{1,0:T(8,128)(2,1)} %param.8, f32[2048]{0:T(1024)} %param.9, f32[16]{0:T(128)S(1)} %add_rsqrt_fusion), kind=kOutput, calls=%fused_computation.1 | convolution fusion | flops 33685504 | bytes 2203712 | tf_op jit(solution)/shard_map/dot_general | solution.py:113
  11.7 0.1 multiply_cosine_fusion.1
  11.8 0.1 multiply_subtract_fusion
  11.9 0.1 maximum_convert_fusion
  12.0 0.2 convolution_convert_fusion
  12.3 0.1 add_compare_fusion
  12.4 1.7 %fusion.55 = (f32[184,2]{1,0:T(8,128)S(1)}, f32[184,2,16]{2,1,0:T(2,128)S(1)}) fusion(bf16[184,2,128]{2,1,0:T(2,128)(2,1)S(1)} %reshape.207, bf16[184,16,256]{2,1,0:T(8,128)(2,1)} %bitcast.55, pred[184,16]{1,0:T(8,128)(4,1)S(1)} %add_compare_fusion), kind=kOutput, calls=%fused_computation.105 | convolution fusion | flops 1524624 | bytes 875840 | tf_op jit(solution)/shard_map/pjc,ptc->pjt/dot_general | solution.py:56
  14.1 0.0 copy-start.1
  14.1 0.1 copy.16
  14.2 0.1 fusion.35
  14.3 0.1 maximum_bitcast_fusion
  14.4 0.1 fusion.42
  14.5 0.1 copy.21
  14.6 0.1 select_reduce_fusion.1
  14.7 0.4 fusion.28
  15.1 0.0 copy-start.2
  15.1 1.6 %fusion.9 = f32[184,2,128]{2,1,0:T(2,128)S(1)} fusion(bf16[184,16,256]{2,1,0:T(8,128)(2,1)} %bitcast.56, f32[184,2,16]{2,1,0:T(2,128)S(1)} %get-tuple-element.18, f32[184,2]{1,0:T(8,128)S(1)} %fusion.28), kind=kOutput, calls=%fused_computation.17 | convolution fusion | flops 1519104 | bytes 967104 | tf_op jit(solution)/shard_map/pjt,ptc->pjc/dot_general | solution.py:73
  16.7 0.0 copy-start.3
  16.7 0.5 fusion.18
  17.2 0.3 convolution_add_fusion.1
  17.5 0.2 fusion.5
  17.8 0.0 copy-done.1
  17.8 0.9 fusion.6
  18.7 0.0 all-reduce.2.cloned.1.call-update
  18.7 0.0 all-gather.2.cloned.1.call-start
  18.7 24.2 %all-reduce.2.cloned.1.call-done = f32[16,2048]{1,0:T(8,128)} async-done(((f32[16,2048]{1,0:T(8,128)}), f32[16,2048]{1,0:T(8,128)}) %all-reduce.2.cloned.1.call-update) | async-done | bytes 131088 | tf_op jit(solution)/shard_map/psum | solution.py:123
  43.0 0.0 copy-done.2
  43.0 1.5 %fusion.17 = bf16[16,2048]{1,0:T(8,128)(2,1)} fusion(f32[16,2048]{1,0:T(8,128)} %all-reduce.2.cloned.1.call-done, bf16[16,2048]{1,0:T(8,128)(2,1)S(1)} %copy-done.2), kind=kLoop, calls=%fused_computation.30 | loop fusion | flops 98304 | bytes 262144 | tf_op jit(solution)/shard_map/convert_element_type | solution.py:124
  44.5 0.0 all-gather.2.cloned.1.call-update
  44.6 0.0 copy-done.3
  44.6 38.5 %all-gather.2.cloned.1.call-done = bf16[256,2048]{1,0:T(8,128)(2,1)} async-done(((bf16[16,2048]{1,0:T(8,128)(2,1)}), bf16[256,2048]{1,0:T(8,128)(2,1)}) %all-gather.2.cloned.1.call-update) | async-done | bytes 1048592 | tf_op jit(solution)/shard_map/all_gather | solution.py:101
  83.1 2.0 %gather_fusion = bf16[16,2048]{1,0:T(8,128)(2,1)S(1)} fusion(bf16[256,2048]{1,0:T(8,128)(2,1)} %all-gather.2.cloned.1.call-done, s32[1024]{0:T(1024)S(1)} %pad_clamp_fusion), kind=kCustom, calls=%fused_computation | custom fusion | bytes 131136 | tf_op jit(solution)/shard_map/jit(_take)/gather | solution.py:104
  85.1 0.7 broadcast_select_fusion
  (12 shorter events, 0.1 us)
Async XLA Ops:
  6.5 3.9 %copy-start = (bf16[2048,1,512]{2,0,1:T(8,128)(2,1)S(1)}, bf16[2048,1,512]{2,0,1:T(8,128)(2,1)}, u32[]{:S(2)}) copy-start(bf16[2048,1,512]{2,0,1:T(8,128)(2,1)} %param.10) | copy-start | bytes 6291460
  6.5 36.4 %all-reduce.2.cloned.1.call-start = ((), (), s32[]{:S(2)}) async-start(), calls=%async_computation | async-start | bytes 262144 | tf_op jit(solution)/shard_map/psum | solution.py:123
  14.1 3.7 %copy-start.1 = (bf16[1,256,2048]{2,1,0:T(8,128)(2,1)S(1)}, bf16[1,256,2048]{2,1,0:T(8,128)(2,1)}, u32[]{:S(2)}) copy-start(bf16[1,256,2048]{2,1,0:T(8,128)(2,1)} %param.11) | copy-start | bytes 3145732
  15.1 27.9 %copy-start.2 = (bf16[16,2048]{1,0:T(8,128)(2,1)S(1)}, bf16[16,2048]{1,0:T(8,128)(2,1)}, u32[]{:S(2)}) copy-start(bf16[16,2048]{1,0:T(8,128)(2,1)} %param.8) | copy-start | bytes 196612
  16.7 27.9 %copy-start.3 = (s32[16]{0:T(128)S(1)}, s32[16]{0:T(128)}, u32[]{:S(2)}) copy-start(s32[16]{0:T(128)} %param.15) | copy-start | bytes 196
  18.7 64.4 %all-gather.2.cloned.1.call-start = ((), (), s32[]{:S(2)}) async-start(), calls=%async_computation.1 | async-start | bytes 1114112 | tf_op jit(solution)/shard_map/all_gather | solution.py:101
Sparse Core Ops, SparseCore 0:
  18.8 24.1 all-reduce.1
  45.1 37.9 all-gather.1
where the time goes:
time: 93.1 us; the launch traced here: 92.7 us
  waiting for transfers between devices  62.8 us (67%)
  between operations  13.6 us (15%)
  other arithmetic  7.4 us (8%)
  matrix products  6.65 us (7%)
  local copies, waits for them, and re-layouts  2.24 us (2%)
    all_gather x1, waiting for transfers between devices, relocate(): collected = lax.all_gather(mixed, 'req', axis=0, tiled=True)  38.5 us
    psum x1, waiting for transfers between devices, local(): summed = lax.psum(partial_out, 'tp')  24.2 us
    gather x1, local copies, waits for them, and re-layouts, relocate(): return jnp.take(collected, source_rows, axis=0)  2.02 us
  transfers between devices with their start and end apart: 2, of which 2 were waited for; matrix products, arithmetic and copies ran while one was open for 0% of the time, Pallas kernels for 0%

commit v1 on v0

--- a/solution.py
+++ b/solution.py
@@ -120,7 +120,7 @@
     new_value = proj[:, (group_size + 1) * head_size :].astype(jnp.bfloat16)
     attn = attend(query, new_key, new_value, kv_cache[:, 0], lengths, page_table)
     partial_out = jnp.dot(attn, w_out[0], preferred_element_type=jnp.float32)
-    summed = lax.psum(partial_out, "tp")
+    summed = jnp.sum(lax.all_gather(partial_out, "tp"), axis=0)
     mixed = (state.astype(jnp.float32) + summed).astype(jnp.bfloat16)
     return relocate(mixed, dest_slot)
 

time: 93.1 us -> 75.3 us (0.81)
  waiting for transfers between devices: 62.8 us -> 39.5 us
  blocking collectives: 0 us -> 7.11 us
    psum x1 -> x0, waiting for transfers between devices: 24.2 us -> none  [local(): summed = lax.psum(partial_out, 'tp')]
    all_gather x0 -> x1, blocking collectives: none -> 7.11 us  [local(): summed = jnp.sum(lax.all_gather(partial_out, 'tp'), axis=0)]
    all_gather x1, waiting for transfers between devices: 38.5 us -> 39.5 us  [relocate(): collected = lax.all_gather(mixed, 'req', axis=0, tiled=True)]
  transfers between devices with their start and end apart: 2 -> 1, of which waited for: 2 -> 1; matrix products, arithmetic and copies ran while one was open for 0% -> 0% of each run, Pallas kernels for 0% -> 0%
where the time goes in v1:
time: 75.3 us; the launch traced here: 75 us
  waiting for transfers between devices  39.5 us (52%)
  between operations  13.6 us (18%)
  blocking collectives  7.11 us (9%)
  other arithmetic  6.51 us (9%)
  matrix products  5.97 us (8%)
  local copies, waits for them, and re-layouts  2.24 us (3%)
    all_gather x1, waiting for transfers between devices, relocate(): collected = lax.all_gather(mixed, 'req', axis=0, tiled=True)  39.5 us
    all_gather x1, blocking collectives, local(): summed = jnp.sum(lax.all_gather(partial_out, 'tp'), axis=0)  7.11 us
    gather x1, local copies, waits for them, and re-layouts, relocate(): return jnp.take(collected, source_rows, axis=0)  2.02 us
    dot_general x1, matrix products, attend(): jnp.einsum('pjc,ptc->pjt', page_query, page_pool[:, :, :head_size], prefe...  1.71 us
    dot_general x1, matrix products, attend(): jnp.einsum('pjt,ptc->pjc', weights.astype(jnp.bfloat16), page_pool[:, :,...  1.54 us
  transfers between devices with their start and end apart: 1, of which 1 were waited for; matrix products, arithmetic and copies ran while one was open for 0% of the time, Pallas kernels for 0%

profile of v1, /device:TPU:0, one launch (start us, length us, event | category | flops | bytes accessed | tf_op | source)
XLA Modules:
  0.0 75.0 jit_solution(329618740508900567)
XLA Ops:
  6.5 0.0 copy-start
  6.5 0.0 all-gather.3.cloned.1.call-start
  6.6 0.8 %fusion.54 = (f32[16]{0:T(128)S(1)}, s32[16]{0:T(128)S(1)}) fusion(s32[16]{0:T(128)} %param.13), kind=kLoop, calls=%fused_computation.104 | loop fusion | flops 272 | bytes 192 | tf_op jit(solution)/shard_map/convert_element_type | solution.py:18
  7.4 0.1 iota_compare_fusion.1
  7.5 1.2 %select_reduce_fusion = (s32[184]{0:T(256)S(1)}, s32[16,184]{1,0:T(8,128)S(1)}) fusion(s32[64]{0:T(128)S(1)} %iota_multiply_fusion, s32[16,64]{1,0:T(8,128)} %param.14, pred[16,64]{1,0:T(8,128)(4,1)S(1)} %iota_compare_fusion.1), kind=kLoop, calls=%fused_computation.13 | loop fusion | flops 1127368 | bytes 17888 | tf_op jit(solution)/shard_map/reduce_sum | solution.py:44
  8.7 0.7 multiply_reduce_fusion
  9.4 1.0 %fusion.14 = f32[16]{0:T(128)S(1)} fusion(bf16[16,2048]{1,0:T(8,128)(2,1)} %param.8), kind=kLoop, calls=%fused_computation.27 | loop fusion | flops 98288 | bytes 65600 | tf_op jit(solution)/shard_map/reduce_sum | solution.py:9
  10.4 0.0 copy-done
  10.4 1.3 %fusion = f32[16,512]{1,0:T(8,128)S(1)} fusion(bf16[2048,1,512]{2,0,1:T(8,128)(2,1)S(1)} %copy-done, bf16[16,2048]{1,0:T(8,128)(2,1)} %param.8, f32[2048]{0:T(1024)} %param.9, f32[16]{0:T(128)S(1)} %add_rsqrt_fusion), kind=kOutput, calls=%fused_computation.1 | convolution fusion | flops 33685504 | bytes 2203712 | tf_op jit(solution)/shard_map/dot_general | solution.py:113
  11.7 0.1 multiply_cosine_fusion.1
  11.8 0.1 multiply_subtract_fusion
  11.9 0.1 maximum_convert_fusion
  12.0 0.2 convolution_convert_fusion
  12.3 0.1 add_compare_fusion
  12.4 1.7 %fusion.55 = (f32[184,2]{1,0:T(8,128)S(1)}, f32[184,2,16]{2,1,0:T(2,128)S(1)}) fusion(bf16[184,2,128]{2,1,0:T(2,128)(2,1)S(1)} %reshape.207, bf16[184,16,256]{2,1,0:T(8,128)(2,1)} %bitcast.57, pred[184,16]{1,0:T(8,128)(4,1)S(1)} %add_compare_fusion), kind=kOutput, calls=%fused_computation.105 | convolution fusion | flops 1524624 | bytes 875840 | tf_op jit(solution)/shard_map/pjc,ptc->pjt/dot_general | solution.py:56
  14.1 0.0 copy-start.1
  14.1 0.1 copy.16
  14.2 0.1 fusion.35
  14.3 0.1 maximum_bitcast_fusion
  14.4 0.1 fusion.42
  14.5 0.1 copy.21
  14.6 0.1 select_reduce_fusion.1
  14.7 0.4 fusion.28
  15.1 1.5 %fusion.9 = f32[184,2,128]{2,1,0:T(2,128)S(1)} fusion(bf16[184,16,256]{2,1,0:T(8,128)(2,1)} %bitcast.58, f32[184,2,16]{2,1,0:T(2,128)S(1)} %get-tuple-element.18, f32[184,2]{1,0:T(8,128)S(1)} %fusion.28), kind=kOutput, calls=%fused_computation.17 | convolution fusion | flops 1519104 | bytes 967104 | tf_op jit(solution)/shard_map/pjt,ptc->pjc/dot_general | solution.py:73
  16.6 0.0 copy-start.2
  16.7 0.0 copy-start.3
  16.7 0.5 fusion.18
  17.2 0.3 convolution_add_fusion.1
  17.5 0.2 fusion.5
  17.7 0.0 copy-done.1
  17.7 0.3 fusion.6
  18.0 7.1 %all-gather = f32[32,2048]{1,0:T(8,128)S(1)} all-gather(f32[16,2048]{1,0:T(8,128)S(1)} %fusion.6), channel_id=2, replica_groups=mesh['req'=16,'tp'=2] {'tp'}, dimensions={0}, use_global_device_ids=true | all-gather | bytes 393216 | tf_op jit(solution)/shard_map/all_gather | solution.py:123
  25.1 0.0 copy-done.2
  25.1 0.6 fusion.17
  25.8 0.0 all-gather.3.cloned.1.call-update
  25.8 0.0 copy-done.3
  25.9 39.5 %all-gather.3.cloned.1.call-done = bf16[256,2048]{1,0:T(8,128)(2,1)} async-done(((bf16[16,2048]{1,0:T(8,128)(2,1)}), bf16[256,2048]{1,0:T(8,128)(2,1)}) %all-gather.3.cloned.1.call-update) | async-done | bytes 1048592 | tf_op jit(solution)/shard_map/all_gather | solution.py:101
  65.4 2.0 %gather_fusion = bf16[16,2048]{1,0:T(8,128)(2,1)S(1)} fusion(bf16[256,2048]{1,0:T(8,128)(2,1)} %all-gather.3.cloned.1.call-done, s32[1024]{0:T(1024)S(1)} %pad_clamp_fusion), kind=kCustom, calls=%fused_computation | custom fusion | bytes 131136 | tf_op jit(solution)/shard_map/jit(_take)/gather | solution.py:104
  67.4 0.7 broadcast_select_fusion
  (13 shorter events, 0.1 us)
Async XLA Ops:
  6.5 3.9 %copy-start = (bf16[2048,1,512]{2,0,1:T(8,128)(2,1)S(1)}, bf16[2048,1,512]{2,0,1:T(8,128)(2,1)}, u32[]{:S(2)}) copy-start(bf16[2048,1,512]{2,0,1:T(8,128)(2,1)} %param.10) | copy-start | bytes 6291460
  6.5 58.9 %all-gather.3.cloned.1.call-start = ((), (), s32[]{:S(2)}) async-start(), calls=%async_computation | async-start | bytes 1114112 | tf_op jit(solution)/shard_map/all_gather | solution.py:101
  14.1 3.6 %copy-start.1 = (bf16[1,256,2048]{2,1,0:T(8,128)(2,1)S(1)}, bf16[1,256,2048]{2,1,0:T(8,128)(2,1)}, u32[]{:S(2)}) copy-start(bf16[1,256,2048]{2,1,0:T(8,128)(2,1)} %param.11) | copy-start | bytes 3145732
  16.6 8.5 %copy-start.2 = (bf16[16,2048]{1,0:T(8,128)(2,1)S(1)}, bf16[16,2048]{1,0:T(8,128)(2,1)}, u32[]{:S(2)}) copy-start(bf16[16,2048]{1,0:T(8,128)(2,1)} %param.8) | copy-start | bytes 196612
  16.7 9.2 %copy-start.3 = (s32[16]{0:T(128)S(1)}, s32[16]{0:T(128)}, u32[]{:S(2)}) copy-start(s32[16]{0:T(128)} %param.15) | copy-start | bytes 196
Sparse Core Ops, SparseCore 0:
  25.9 39.4 all-gather.2
